TPU v7x, 512 devices: a whole 4x8x8 slice. The times are simulated.
512 devices in a mesh: item: 2 (over core), row: 16 (over y, z_lo), col: 16 (over z_hi, x).
Axes of the slice: x: 4, y: 8, z: 8 (z_hi: 4, z_lo: 2; z = z_hi * 2 + z_lo), core: 2. Of those that a mesh axis runs over, the one named last changes fastest.
Arguments:
- latents: bfloat16 [2, 2, 64, 64, 3072], P('item', None, 'row', 'col'), may hold values from -640 to 640
- prompt_rows: bfloat16 [2, 226, 3072], P('item'), may hold values from -640 to 640
- peg_weight: bfloat16 [3, 3, 3072], replicated, may hold values from -1 to 1
- modulation_weight: bfloat16 [512, 6144], P(None, 'col'), may hold values from -0.5 to 0.5
- qkv_weight: bfloat16 [3072, 3, 2048], P(('item', 'row'), None, 'col'), may hold values from -3 to 3
- text_len: int32 [2], P('item'), may hold values from 56 to 226, as said below
- timestep: int32 [2], P('item'), may hold values from 0 to 999
Outputs:
- attended: bfloat16 [2, 2, 64, 64, 2048], P('item', None, 'row', None, 'col')
Inputs may be any that keep to these rules, and one draw needn't show every extreme that they name: `text_len`: one item has all 226 text tokens valid; the others have fewer.
All inputs are finite; a program needn't handle non-finite values.
Results may differ from a plain program's by a relative error of at most 0.02.
Values may be sent and summed in bfloat16 or wider, within the bound.
No kernel may reach another device: no remote copies, remote signals or barrier semaphores. Data moves between devices by JAX's collectives and lax.ppermute only.
A program may use at most 64 MiB of HBM per device.

v0:
```python
import math
import jax
import jax.numpy as jnp
from jax import lax
from jax.sharding import PartitionSpec as P

HD = 64


def with_halo(block, sides, width):
    for axis, dim in sides:
        count = lax.axis_size(axis)
        forward = [(i, i + 1) for i in range(count - 1)]
        backward = [(target, source) for source, target in forward]
        low = lax.ppermute(
            lax.slice_in_dim(block, block.shape[dim] - width, None, axis=dim), axis, forward
        )
        high = lax.ppermute(lax.slice_in_dim(block, 0, width, axis=dim), axis, backward)
        block = jnp.concatenate([low, block, high], axis=dim)
    return block


def time_angles(step, count):
    half = count // 2
    freqs = jnp.exp(-math.log(10000.0) * jnp.arange(half, dtype=jnp.float32) / half)
    angle = step.astype(jnp.float32) * freqs
    return jnp.concatenate([jnp.cos(angle), jnp.sin(angle)])


def modulate(rows, shift, scale):
    values = rows.astype(jnp.float32)
    center = jnp.mean(values, axis=-1, keepdims=True)
    centered = values - center
    spread = jnp.mean(centered * centered, axis=-1, keepdims=True)
    return (centered * lax.rsqrt(spread + 1e-06) * (1.0 + scale) + shift).astype(jnp.bfloat16)


def absorb(carry, queries, key_rows, value_rows, valid):
    running_max, running_sum, weighted = carry
    count = key_rows.shape[0]
    heads = queries.shape[1]
    key_heads = key_rows.reshape(count, heads, HD)
    value_heads = value_rows.reshape(count, heads, HD)
    scores = (
        jnp.einsum("rhd,bhd->rhb", queries, key_heads, preferred_element_type=jnp.float32) * 0.125
    )
    if valid is not None:
        scores = jnp.where(valid[None, None, :], scores, -jnp.inf)
    newest = jnp.maximum(running_max, jnp.max(scores, axis=-1))
    weights = jnp.exp(scores - newest[..., None])
    shrink_by = jnp.exp(running_max - newest)
    running_sum = running_sum * shrink_by + jnp.sum(weights, axis=-1)
    weighted = weighted * shrink_by[..., None] + jnp.einsum(
        "rhb,bhd->rhd",
        weights.astype(jnp.bfloat16),
        value_heads,
        preferred_element_type=jnp.float32,
    )
    return (newest, running_sum, weighted)


def on_device(latents, prompt_rows, peg_weight, modulation_weight, qkv_weight, text_len, timestep):
    tile_h = latents.shape[2]
    tile_w = latents.shape[3]
    width = latents.shape[4]
    padded = with_halo(latents, (("row", 2), ("col", 3)), 1)
    summed = latents.astype(jnp.float32)
    for row_tap in range(3):
        for col_tap in range(3):
            summed = summed + padded[
                :, :, row_tap : row_tap + tile_h, col_tap : col_tap + tile_w, :
            ].astype(jnp.float32) * peg_weight[row_tap, col_tap].astype(jnp.float32)
    convolved = summed.astype(jnp.bfloat16)
    activation = jax.nn.silu(time_angles(timestep[0], modulation_weight.shape[0])).astype(
        jnp.bfloat16
    )
    own_columns = jnp.dot(
        activation[None, :], modulation_weight, preferred_element_type=jnp.float32
    )
    modulation = lax.all_gather(own_columns, "col", axis=1, tiled=True)[0]
    shift = modulation[:width]
    scale = modulation[width:]
    group_rows = lax.all_gather(modulate(convolved, shift, scale), "col", axis=3, tiled=True)
    frames = group_rows.shape[1]
    grid_w = group_rows.shape[3]
    flat_rows = group_rows.reshape(-1, width)
    row_count = flat_rows.shape[0]
    text_normed = modulate(prompt_rows[0], shift, scale)
    text_count = text_normed.shape[0]
    head_width = qkv_weight.shape[2]
    full_weight = lax.all_gather(qkv_weight, ("item", "row"), axis=0, tiled=True)
    latent_proj = jnp.einsum(
        "rd,dkc->rkc", flat_rows, full_weight, preferred_element_type=jnp.float32
    )
    text_proj = jnp.einsum(
        "rd,dkc->rkc", text_normed, full_weight, preferred_element_type=jnp.float32
    )
    latent_qkv = latent_proj.astype(jnp.bfloat16)
    text_qkv = text_proj.astype(jnp.bfloat16)
    heads = head_width // HD
    queries = latent_qkv[:, 0, :].reshape(row_count, heads, HD)
    local_keys = latent_qkv[:, 1, :]
    local_values = latent_qkv[:, 2, :]
    text_valid = jnp.arange(text_count, dtype=jnp.int32) < text_len[0]
    start_carry = (
        jnp.full((row_count, heads), -jnp.inf, jnp.float32),
        jnp.zeros((row_count, heads), jnp.float32),
        jnp.zeros((row_count, heads, HD), jnp.float32),
    )
    text_carry = absorb(start_carry, queries, text_qkv[:, 1, :], text_qkv[:, 2, :], text_valid)
    key_rows = lax.all_gather(local_keys, "row", axis=0, tiled=True)
    value_rows = lax.all_gather(local_values, "row", axis=0, tiled=True)
    total_rows = key_rows.shape[0]
    block_count = total_rows // row_count

    def one_block(state, pair):
        return (absorb(state, queries, pair[0], pair[1], None), None)

    state, unused = lax.scan(
        one_block,
        text_carry,
        (
            key_rows.reshape(block_count, row_count, head_width),
            value_rows.reshape(block_count, row_count, head_width),
        ),
    )
    running_max, running_sum, weighted = state
    attended = (weighted / running_sum[..., None]).astype(jnp.bfloat16)
    return attended.reshape(1, frames, tile_h, grid_w, head_width)


def solution(mesh):
    in_specs = (
        P("item", None, "row", "col", None),
        P("item", None, None),
        P(),
        P(None, "col"),
        P(("item", "row"), None, "col"),
        P("item"),
        P("item"),
    )
    out_specs = P("item", None, "row", None, "col")
    return jax.shard_map(
        on_device, mesh=mesh, in_specs=in_specs, out_specs=out_specs, check_vma=False
    )
```

profile of v0, /device:TPU:6, one launch (start us, length us, event | category | flops | bytes accessed | tf_op | source)
XLA Modules:
  0.0 427.7 jit_solution(11197046939042537317)
XLA Ops:
  6.5 1.1 copy.22
  7.8 1.3 collective-permute-start.1
  9.1 4.9 %collective-permute-start = (bf16[1,2,1,4,3072]{4,2,1,0,3:T(2,128)(2,1)S(1)}, bf16[1,2,1,4,3072]{4,2,1,0,3:T(2,128)(2,1)S(1)}, u32[]{:S(2)}, u32[]{:S(2)}) collective-permute-start(bf16[1,2,1,4,3072]{4,2,1,0,3:T(2,128)(2,1)S(1)} %get-tuple-element.95), channel_id=1, source_target_pairs={{0,16},{16,32},{32,48},{48,64},{64,80},{80,96},{96,112},{112,128},... | collective-permute-start | bytes 147464 | tf_op jit(solution)/shard_map/ppermute | solution.py:15
  14.7 1.0 slice_convert_fusion.8
  15.9 39.2 %all-gather.3 = f32[16,1,384]{2,1,0:T(1,128)S(1)} all-gather(f32[1,1,384]{2,1,0:T(1,128)S(1)} %convolution_bitcast_fusion.2), channel_id=2, replica_groups=mesh['item'=2,'row'=16,'col'=16] {'col'}, dimensions={0}, use_global_device_ids=true | all-gather | bytes 26112 | tf_op jit(solution)/shard_map/all_gather | solution.py:80
  55.2 6.1 %collective-permute-start.2 = (bf16[1,2,6,1,3072]{4,2,1,0,3:T(8,128)(2,1)S(1)}, bf16[1,2,6,1,3072]{4,2,1,0,3:T(8,128)(2,1)S(1)}, u32[]{:S(2)}, u32[]{:S(2)}) collective-permute-start(bf16[1,2,6,1,3072]{4,2,1,0,3:T(8,128)(2,1)S(1)} %get-tuple-element.93), channel_id=1, source_target_pairs={{0,1},{1,2},{2,3},{3,4},{4,5},{5,6},{6,7},{7,8},{8,9},{9,10},{10,1... | collective-permute-start | bytes 221192 | tf_op jit(solution)/shard_map/ppermute | solution.py:15
  61.4 3.1 collective-permute-start.3
  64.5 0.6 collective-permute-done.2
  65.1 5.7 %collective-permute-done.3 = bf16[1,2,6,1,3072]{4,2,1,0,3:T(8,128)(2,1)S(1)} collective-permute-done((bf16[1,2,6,1,3072]{4,2,1,0,3:T(8,128)(2,1)S(1)}, bf16[1,2,6,1,3072]{4,2,1,0,3:T(8,128)(2,1)S(1)}, u32[]{:S(2)}, u32[]{:S(2)}) %collective-permute-start.3) | collective-permute-done | bytes 73760 | tf_op jit(solution)/shard_map/ppermute | solution.py:18
  70.9 0.6 maximum_maximum_fusion
  71.5 1.4 convert_reduce_fusion.1
  73.1 0.9 fusion.37
  74.1 0.7 all-gather.9.cloned.1.call-update
  74.8 77.8 %all-gather.11.cloned.1.call-done = bf16[1,2,4,64,3072]{4,2,1,0,3:T(4,128)(2,1)} async-done(((bf16[1,2,4,4,3072]{4,2,1,0,3:T(4,128)(2,1)}), bf16[1,2,4,64,3072]{4,2,1,0,3:T(4,128)(2,1)}) %all-gather.11.cloned.1.call-update) | async-done | bytes 3145744 | tf_op jit(solution)/shard_map/all_gather | solution.py:83
  152.7 5.3 %copy.28 = bf16[1,2,4,64,3072]{4,3,2,1,0:T(8,128)(2,1)} copy(bf16[1,2,4,64,3072]{4,2,1,0,3:T(4,128)(2,1)} %all-gather.11.cloned.1.call-done) | data formatting | bytes 6291456 | tf_op jit(solution)/shard_map/all_gather | solution.py:83
  158.0 62.5 %all-gather.9.cloned.1.call-done = bf16[3072,3,128]{2,0,1:T(8,128)(2,1)} async-done(((bf16[96,3,128]{2,0,1:T(8,128)(2,1)}), bf16[3072,3,128]{2,0,1:T(8,128)(2,1)}) %all-gather.9.cloned.1.call-update) | async-done | bytes 2359312 | tf_op jit(solution)/shard_map/all_gather | solution.py:91
  220.5 4.1 convolution_convert_fusion
  224.6 0.7 fusion.52
  227.0 0.5 fusion.11
  227.6 1.1 fusion.24
  229.7 71.5 %all-gather.13.cloned.1.call-done = bf16[8192,1,128]{0,2,1:T(8,128)(2,1)} async-done(((bf16[512,1,128]{0,2,1:T(8,128)(2,1)}), bf16[8192,1,128]{0,2,1:T(8,128)(2,1)}) %all-gather.13.cloned.1.call-update) | async-done | bytes 2097168 | tf_op jit(solution)/shard_map/all_gather | solution.py:111
  301.2 2.4 copy.35
  303.6 1.2 copy.30
  304.8 72.2 %all-gather.15.cloned.1.call-done = bf16[8192,1,128]{0,2,1:T(8,128)(2,1)} async-done(((bf16[512,1,128]{0,2,1:T(8,128)(2,1)}), bf16[8192,1,128]{0,2,1:T(8,128)(2,1)}) %all-gather.15.cloned.1.call-update) | async-done | bytes 2097168 | tf_op jit(solution)/shard_map/all_gather | solution.py:112
  377.0 2.4 copy.36
  379.5 2.5 copy.31
  382.0 38.1 %while.14 = (s32[]{:T(128)}, f32[512,2]{0,1:T(2,128)S(1)}, f32[512,2]{0,1:T(2,128)S(1)}, f32[512,2,64]{0,2,1:T(8,128)S(1)}, bf16[16,512,128]{1,2,0:T(8,128)(2,1)...) while((s32[]{:T(128)}, f32[512,2]{0,1:T(2,128)S(1)}, ...), condition=%wide.region_9.10_spmd, body=%wide.region_6.9_spmd.sunk | while | flops 138545152 | bytes 7798881 | solution.py:119
  382.0 0.9 constant_dynamic-slice_fusion.3
  384.3 0.9 constant_dynamic-slice_fusion.3
  386.7 0.9 constant_dynamic-slice_fusion.3
  388.6 0.5 fusion.78
  389.1 0.9 constant_dynamic-slice_fusion.3
  391.5 0.9 constant_dynamic-slice_fusion.3
  393.9 0.9 constant_dynamic-slice_fusion.3
  396.2 0.9 constant_dynamic-slice_fusion.3
  398.1 0.5 fusion.78
  398.6 0.9 constant_dynamic-slice_fusion.3
  400.5 0.5 fusion.78
  401.0 0.9 constant_dynamic-slice_fusion.3
  402.9 0.5 fusion.78
  403.4 0.9 constant_dynamic-slice_fusion.3
  405.8 0.9 constant_dynamic-slice_fusion.3
  408.2 0.9 constant_dynamic-slice_fusion.3
  410.5 0.9 constant_dynamic-slice_fusion.3
  412.9 0.9 constant_dynamic-slice_fusion.3
  415.3 0.9 constant_dynamic-slice_fusion.3
  417.7 0.9 constant_dynamic-slice_fusion.3
  420.3 0.8 copy.34
  (130 shorter events, 23.6 us)
Async XLA Ops:
  6.5 9.2 %copy-start = (bf16[512,384]{1,0:T(8,128)(2,1)S(1)}, bf16[512,384]{1,0:T(8,128)(2,1)}, u32[]{:S(2)}) copy-start(bf16[512,384]{1,0:T(8,128)(2,1)} %param.12) | copy-start | bytes 1179652
  6.5 146.1 %all-gather.11.cloned.1.call-start = ((), (), s32[]{:S(2)}) async-start(), calls=%async_computation.1 | async-start | bytes 3342336 | tf_op jit(solution)/shard_map/all_gather | solution.py:83
  7.8 47.3 %collective-permute-start.1 = (bf16[1,2,1,4,3072]{4,2,1,0,3:T(2,128)(2,1)S(1)}, bf16[1,2,1,4,3072]{4,2,1,0,3:T(2,128)(2,1)S(1)}, u32[]{:S(2)}, u32[]{:S(2)}) collective-permute-start(bf16[1,2,1,4,3072]{4,2,1,0,3:T(2,128)(2,1)S(1)} %get-tuple-element.96), channel_id=1, source_target_pairs={{16,0},{32,16},{48,32},{64,48},{80,64},{96,80},{112,96},{128,112},... | collective-permute-start | bytes 147464 | tf_op jit(solution)/shard_map/ppermute | solution.py:18
  9.1 46.0 %collective-permute-start = (bf16[1,2,1,4,3072]{4,2,1,0,3:T(2,128)(2,1)S(1)}, bf16[1,2,1,4,3072]{4,2,1,0,3:T(2,128)(2,1)S(1)}, u32[]{:S(2)}, u32[]{:S(2)}) collective-permute-start(bf16[1,2,1,4,3072]{4,2,1,0,3:T(2,128)(2,1)S(1)} %get-tuple-element.95), channel_id=1, source_target_pairs={{0,16},{16,32},{32,48},{48,64},{64,80},{80,96},{96,112},{112,128},... | collective-permute-start | bytes 147464 | tf_op jit(solution)/shard_map/ppermute | solution.py:15
  55.2 9.9 %collective-permute-start.2 = (bf16[1,2,6,1,3072]{4,2,1,0,3:T(8,128)(2,1)S(1)}, bf16[1,2,6,1,3072]{4,2,1,0,3:T(8,128)(2,1)S(1)}, u32[]{:S(2)}, u32[]{:S(2)}) collective-permute-start(bf16[1,2,6,1,3072]{4,2,1,0,3:T(8,128)(2,1)S(1)} %get-tuple-element.93), channel_id=1, source_target_pairs={{0,1},{1,2},{2,3},{3,4},{4,5},{5,6},{6,7},{7,8},{8,9},{9,10},{10,1... | collective-permute-start | bytes 221192 | tf_op jit(solution)/shard_map/ppermute | solution.py:15
  61.4 9.5 %collective-permute-start.3 = (bf16[1,2,6,1,3072]{4,2,1,0,3:T(8,128)(2,1)S(1)}, bf16[1,2,6,1,3072]{4,2,1,0,3:T(8,128)(2,1)S(1)}, u32[]{:S(2)}, u32[]{:S(2)}) collective-permute-start(bf16[1,2,6,1,3072]{4,2,1,0,3:T(8,128)(2,1)S(1)} %get-tuple-element.94), channel_id=1, source_target_pairs={{1,0},{2,1},{3,2},{4,3},{5,4},{6,5},{7,6},{8,7},{9,8},{10,9},{11,1... | collective-permute-start | bytes 221192 | tf_op jit(solution)/shard_map/ppermute | solution.py:18
  74.0 146.4 %all-gather.9.cloned.1.call-start = ((), (), s32[]{:S(2)}) async-start(), calls=%async_computation | async-start | bytes 2433024 | tf_op jit(solution)/shard_map/all_gather | solution.py:91
  74.8 226.4 %all-gather.13.cloned.1.call-start = ((), (), s32[]{:S(2)}) async-start(), calls=%async_computation.2 | async-start | bytes 2228224 | tf_op jit(solution)/shard_map/all_gather | solution.py:111
  220.5 6.3 %copy-start.1 = (bf16[1,226,3072]{2,1,0:T(8,128)(2,1)S(1)}, bf16[1,226,3072]{2,1,0:T(8,128)(2,1)}, u32[]{:S(2)}) copy-start(bf16[1,226,3072]{2,1,0:T(8,128)(2,1)} %param.10) | copy-start | bytes 4165636
  225.4 151.7 %all-gather.15.cloned.1.call-start = ((), (), s32[]{:S(2)}) async-start(), calls=%async_computation.3 | async-start | bytes 2228224 | tf_op jit(solution)/shard_map/all_gather | solution.py:112
  225.9 1.7 copy-start.2
Sparse Core Ops, SparseCore 0:
  74.2 78.4 all-gather.10
  154.8 65.5 all-gather.8
  225.5 75.6 all-gather.12
  303.2 73.8 all-gather.14
where the time goes:
time: 428 us
  waiting for transfers between devices  291 us (68%)
  blocking collectives  39.2 us (9%)
  local copies, waits for them, and re-layouts  31.9 us (7%)
  matrix products  22.3 us (5%)
  starting transfers between devices  15.8 us (4%)
  between operations  14.8 us (3%)
  other arithmetic  11.6 us (3%)
    all_gather x1, waiting for transfers between devices, on_device(): lax.all_gather(modulate(convolved, shift, scale), 'col', axis=3, tiled=True)  77.8 us
    all_gather x1, waiting for transfers between devices, on_device(): value_rows = lax.all_gather(local_values, 'row', axis=0, tiled=True)  72.2 us
    all_gather x1, waiting for transfers between devices, on_device(): key_rows = lax.all_gather(local_keys, 'row', axis=0, tiled=True)  71.5 us
    all_gather x1, waiting for transfers between devices, on_device(): lax.all_gather(qkv_weight, ('item', 'row'), axis=0, tiled=True)  62.5 us
    all_gather x1, blocking collectives, on_device(): modulation = lax.all_gather(own_columns, 'col', axis=1, tiled=True)[0]  39.2 us
    dynamic_slice x16, local copies, waits for them, and re-layouts, on_device(): lax.scan(one_block, text_carry, (key_rows.reshape(block_count, row_count,...  14.8 us
    ppermute x2, starting transfers between devices, with_halo(): lax.ppermute(lax.slice_in_dim(block, block.shape[dim] - width, None, axis...  11 us
  transfers between devices with their start and end apart: 8, of which 6 were waited for; matrix products, arithmetic and copies ran while one was open for 3% of the time, Pallas kernels for 0%

commit v1 on v0

--- a/solution.py
+++ b/solution.py
@@ -80,7 +80,9 @@
     modulation = lax.all_gather(own_columns, "col", axis=1, tiled=True)[0]
     shift = modulation[:width]
     scale = modulation[width:]
-    group_rows = lax.all_gather(modulate(convolved, shift, scale), "col", axis=3, tiled=True)
+    part = modulate(convolved, shift, scale)
+    repeated = jnp.stack([part] * lax.axis_size("col"))
+    group_rows = jnp.concatenate(lax.all_to_all(repeated, "col", 0, 0), axis=3)
     frames = group_rows.shape[1]
     grid_w = group_rows.shape[3]
     flat_rows = group_rows.reshape(-1, width)

time: 428 us -> 380 us (0.89)
  waiting for transfers between devices: 291 us -> 226 us
  starting transfers between devices: 15.8 us -> 26.1 us
  local copies, waits for them, and re-layouts: 31.9 us -> 39.5 us
    all_gather x1 -> x0, waiting for transfers between devices: 77.8 us -> none  [on_device(): lax.all_gather(modulate(convolved, shift, scale), 'col', axis=3, tiled=True)]
    all_to_all x0 -> x1, waiting for transfers between devices: none -> 72.5 us  [on_device(): group_rows = jnp.concatenate(lax.all_to_all(repeated, 'col', 0, 0), axis=3)]
    all_gather x1, waiting for transfers between devices: 62.5 us -> 1.12 us  [on_device(): lax.all_gather(qkv_weight, ('item', 'row'), axis=0, tiled=True)]
    all_to_all x0 -> x1, starting transfers between devices: none -> 11.1 us  [on_device(): group_rows = jnp.concatenate(lax.all_to_all(repeated, 'col', 0, 0), axis=3)]
    another operation x0 -> x2, local copies, waits for them, and re-layouts: none -> 8.95 us  [the longest x1 5.9 us: on_device(): flat_rows = group_rows.reshape(-1, width)]
    all_gather x1 -> x0, local copies, waits for them, and re-layouts: 5.3 us -> none  [on_device(): lax.all_gather(modulate(convolved, shift, scale), 'col', axis=3, tiled=True)]
    ppermute x2, starting transfers between devices: 11 us -> 6.2 us  [with_halo(): lax.ppermute(lax.slice_in_dim(block, block.shape[dim] - width, None, axis...]
    ppermute x2, waiting for transfers between devices: 5.74 us -> 0.91 us  [with_halo(): lax.ppermute(lax.slice_in_dim(block, 0, width, axis=dim), axis, backward)]
  transfers between devices with their start and end apart: 8 -> 8, of which waited for: 6 -> 6; matrix products, arithmetic and copies ran while one was open for 3% -> 5% of each run, Pallas kernels for 0% -> 0%
where the time goes in v1:
time: 380 us; the launch traced here: 379 us
  waiting for transfers between devices  226 us (59%)
  local copies, waits for them, and re-layouts  39.5 us (10%)
  blocking collectives  38.8 us (10%)
  starting transfers between devices  26.1 us (7%)
  matrix products  22.2 us (6%)
  between operations  14.8 us (4%)
  other arithmetic  10.8 us (3%)
    all_gather x1, waiting for transfers between devices, on_device(): key_rows = lax.all_gather(local_keys, 'row', axis=0, tiled=True)  73.7 us
    all_to_all x1, waiting for transfers between devices, on_device(): group_rows = jnp.concatenate(lax.all_to_all(repeated, 'col', 0, 0), axis=3)  72.5 us
    all_gather x1, waiting for transfers between devices, on_device(): value_rows = lax.all_gather(local_values, 'row', axis=0, tiled=True)  72.4 us
    all_gather x1, blocking collectives, on_device(): modulation = lax.all_gather(own_columns, 'col', axis=1, tiled=True)[0]  38.8 us
    dynamic_slice x16, local copies, waits for them, and re-layouts, on_device(): lax.scan(one_block, text_carry, (key_rows.reshape(block_count, row_count,...  14.8 us
    all_to_all x1, starting transfers between devices, on_device(): group_rows = jnp.concatenate(lax.all_to_all(repeated, 'col', 0, 0), axis=3)  11.1 us
    dot_general x17, matrix products, absorb(): jnp.einsum('rhb,bhd->rhd', weights.astype(jnp.bfloat16), value_heads, pre...  8.55 us
    ppermute x2, starting transfers between devices, with_halo(): lax.ppermute(lax.slice_in_dim(block, 0, width, axis=dim), axis, backward)  8.46 us
  transfers between devices with their start and end apart: 8, of which 6 were waited for; matrix products, arithmetic and copies ran while one was open for 5% of the time, Pallas kernels for 0%

profile of v1, /device:TPU:6, one launch (start us, length us, event | category | flops | bytes accessed | tf_op | source)
XLA Modules:
  0.0 378.9 jit_solution(12872699704868458330)
XLA Ops:
  6.5 0.9 fusion.59
  7.5 4.3 %collective-permute-start = (bf16[1,2,1,4,3072]{4,3,2,1,0:T(4,128)(2,1)S(1)}, bf16[1,2,1,4,3072]{4,3,2,1,0:T(4,128)(2,1)S(1)}, u32[]{:S(2)}, u32[]{:S(2)}) collective-permute-start(bf16[1,2,1,4,3072]{4,3,2,1,0:T(4,128)(2,1)S(1)} %get-tuple-element.94), channel_id=1, source_target_pairs={{0,16},{16,32},{32,48},{48,64},{64,80},{80,96},{96,112},{112,128},... | collective-permute-start | bytes 147464 | tf_op jit(solution)/shard_map/ppermute | solution.py:15
  11.7 1.3 collective-permute-start.1
  13.8 1.0 slice_convert_fusion.8
  15.0 38.8 %all-gather.3 = f32[16,1,384]{2,1,0:T(1,128)S(1)} all-gather(f32[1,1,384]{2,1,0:T(1,128)S(1)} %convolution_bitcast_fusion.2), channel_id=2, replica_groups=mesh['item'=2,'row'=16,'col'=16] {'col'}, dimensions={0}, use_global_device_ids=true | all-gather | bytes 26112 | tf_op jit(solution)/shard_map/all_gather | solution.py:80
  53.8 1.0 constant_dynamic-update-slice_fusion.1
  55.0 7.2 %collective-permute-start.3 = (bf16[1,2,6,1,3072]{4,3,2,1,0:T(2,128)(2,1)S(1)}, bf16[1,2,6,1,3072]{4,3,2,1,0:T(2,128)(2,1)S(1)}, u32[]{:S(2)}, u32[]{:S(2)}) collective-permute-start(bf16[1,2,6,1,3072]{4,3,2,1,0:T(2,128)(2,1)S(1)} %get-tuple-element.92), channel_id=1, source_target_pairs={{1,0},{2,1},{3,2},{4,3},{5,4},{6,5},{7,6},{8,7},{9,8},{10,9},{11,1... | collective-permute-start | bytes 221192 | tf_op jit(solution)/shard_map/ppermute | solution.py:18
  62.2 1.9 collective-permute-start.2
  64.2 0.9 collective-permute-done.3
  65.1 4.2 %collective-permute-done.2 = bf16[1,2,6,1,3072]{4,3,2,1,0:T(2,128)(2,1)S(1)} collective-permute-done((bf16[1,2,6,1,3072]{4,3,2,1,0:T(2,128)(2,1)S(1)}, bf16[1,2,6,1,3072]{4,3,2,1,0:T(2,128)(2,1)S(1)}, u32[]{:S(2)}, u32[]{:S(2)}) %collective-permute-start.2) | collective-permute-done | bytes 73760 | tf_op jit(solution)/shard_map/ppermute | solution.py:15
  69.2 2.0 convert_reduce_fusion.1
  71.8 3.0 stack.2
  74.8 11.1 %all-to-all-start = ((bf16[16,1,2,4,4,3072]{5,4,3,2,1,0:T(4,128)(2,1)}), bf16[16,1,2,4,4,3072]{5,4,3,2,1,0:T(4,128)(2,1)S(1)}, u32[]{:S(2)}, u32[]{:S(2)}) async-start(bf16[16,1,2,4,4,3072]{5,4,3,2,1,0:T(4,128)(2,1)} %stack.2), calls=%async_computation | async-start | bytes 6291456 | tf_op jit(solution)/shard_map/all_to_all | solution.py:85
  86.0 0.7 all-gather.8.cloned.1.call-update
  86.7 72.5 %all-to-all-done = bf16[16,1,2,4,4,3072]{5,4,3,2,1,0:T(4,128)(2,1)S(1)} async-done(((bf16[16,1,2,4,4,3072]{5,4,3,2,1,0:T(4,128)(2,1)}), bf16[16,1,2,4,4,3072]{5,4,3,2,1,0:T(4,128)(2,1)S(1)}, u32[]{:S(2)}, u32[]{:S(2)}) %all-to-all-start) | async-done | bytes 3145760 | tf_op jit(solution)/shard_map/all_to_all | solution.py:85
  159.2 2.9 copy.22
  162.2 5.9 %reshape.200 = bf16[512,3072,1]{1,0,2:T(8,128)(2,1)} reshape(bf16[1,2,4,16,4,3072]{5,4,3,2,1,0:T(4,128)(2,1)} %copy.22) | data formatting | bytes 6291456 | tf_op jit(solution)/shard_map/reshape;reshape | solution.py:88
  168.1 1.1 all-gather.8.cloned.1.call-done
  169.2 4.0 %convolution_convert_fusion = bf16[512,3,128]{0,2,1:T(8,128)(2,1)S(1)} fusion(bf16[512,3072,1]{1,0,2:T(8,128)(2,1)} %reshape.200, bf16[3072,3,128]{2,0,1:T(8,128)(2,1)} %all-gather.8.cloned.1.call-done), kind=kOutput, calls=%fused_computation.32 | convolution fusion | flops 1208156160 | bytes 5898240 | tf_op jit(solution)/shard_map/rd,dkc->rkc/dot_general | solution.py:94
  173.3 0.7 fusion.57
  175.9 0.5 fusion.11
  176.4 1.1 fusion.24
  178.5 73.7 %all-gather.10.cloned.1.call-done = bf16[8192,1,128]{0,2,1:T(8,128)(2,1)} async-done(((bf16[512,1,128]{0,2,1:T(8,128)(2,1)}), bf16[8192,1,128]{0,2,1:T(8,128)(2,1)}) %all-gather.10.cloned.1.call-update) | async-done | bytes 2097168 | tf_op jit(solution)/shard_map/all_gather | solution.py:113
  252.3 2.4 copy.29
  254.7 1.2 copy.24
  255.9 72.4 %all-gather.12.cloned.1.call-done = bf16[8192,1,128]{0,2,1:T(8,128)(2,1)} async-done(((bf16[512,1,128]{0,2,1:T(8,128)(2,1)}), bf16[8192,1,128]{0,2,1:T(8,128)(2,1)}) %all-gather.12.cloned.1.call-update) | async-done | bytes 2097168 | tf_op jit(solution)/shard_map/all_gather | solution.py:114
  328.2 2.4 copy.30
  330.7 2.5 copy.25
  333.2 38.1 %while.14 = (s32[]{:T(128)}, f32[512,2]{0,1:T(2,128)S(1)}, f32[512,2]{0,1:T(2,128)S(1)}, f32[512,2,64]{0,2,1:T(8,128)S(1)}, bf16[16,512,128]{1,2,0:T(8,128)(2,1)...) while((s32[]{:T(128)}, f32[512,2]{0,1:T(2,128)S(1)}, ...), condition=%wide.region_9.10_spmd, body=%wide.region_6.9_spmd.sunk | while | flops 138545152 | bytes 7798881 | solution.py:121
  333.2 0.9 constant_dynamic-slice_fusion.3
  335.5 0.9 constant_dynamic-slice_fusion.3
  337.4 0.5 fusion.84
  337.9 0.9 constant_dynamic-slice_fusion.3
  339.8 0.5 fusion.84
  340.3 0.9 constant_dynamic-slice_fusion.3
  342.7 0.9 constant_dynamic-slice_fusion.3
  345.1 0.9 constant_dynamic-slice_fusion.3
  347.5 0.9 constant_dynamic-slice_fusion.3
  349.8 0.9 constant_dynamic-slice_fusion.3
  352.2 0.9 constant_dynamic-slice_fusion.3
  354.6 0.9 constant_dynamic-slice_fusion.3
  357.0 0.9 constant_dynamic-slice_fusion.3
  359.4 0.9 constant_dynamic-slice_fusion.3
  361.8 0.9 constant_dynamic-slice_fusion.3
  364.1 0.9 constant_dynamic-slice_fusion.3
  366.5 0.9 constant_dynamic-slice_fusion.3
  368.9 0.9 constant_dynamic-slice_fusion.3
  371.5 0.8 copy.28
  (138 shorter events, 24.9 us)
Async XLA Ops:
  6.5 8.2 %copy-start = (bf16[512,384]{1,0:T(8,128)(2,1)S(1)}, bf16[512,384]{1,0:T(8,128)(2,1)}, u32[]{:S(2)}) copy-start(bf16[512,384]{1,0:T(8,128)(2,1)} %param.12) | copy-start | bytes 1179652
  6.5 62.7 %copy-start.2 = (bf16[1,2,4,4,3072]{4,3,2,1,0:T(4,128)(2,1)S(1)}, bf16[1,2,4,4,3072]{4,3,2,1,0:T(4,128)(2,1)}, u32[]{:S(2)}) copy-start(bf16[1,2,4,4,3072]{4,3,2,1,0:T(4,128)(2,1)} %param.9) | copy-start | bytes 589828
  7.5 46.3 %collective-permute-start = (bf16[1,2,1,4,3072]{4,3,2,1,0:T(4,128)(2,1)S(1)}, bf16[1,2,1,4,3072]{4,3,2,1,0:T(4,128)(2,1)S(1)}, u32[]{:S(2)}, u32[]{:S(2)}) collective-permute-start(bf16[1,2,1,4,3072]{4,3,2,1,0:T(4,128)(2,1)S(1)} %get-tuple-element.94), channel_id=1, source_target_pairs={{0,16},{16,32},{32,48},{48,64},{64,80},{80,96},{96,112},{112,128},... | collective-permute-start | bytes 147464 | tf_op jit(solution)/shard_map/ppermute | solution.py:15
  11.7 43.0 %collective-permute-start.1 = (bf16[1,2,1,4,3072]{4,3,2,1,0:T(4,128)(2,1)S(1)}, bf16[1,2,1,4,3072]{4,3,2,1,0:T(4,128)(2,1)S(1)}, u32[]{:S(2)}, u32[]{:S(2)}) collective-permute-start(bf16[1,2,1,4,3072]{4,3,2,1,0:T(4,128)(2,1)S(1)} %get-tuple-element.93), channel_id=1, source_target_pairs={{16,0},{32,16},{48,32},{64,48},{80,64},{96,80},{112,96},{128,112},... | collective-permute-start | bytes 147464 | tf_op jit(solution)/shard_map/ppermute | solution.py:18
  55.0 10.0 %collective-permute-start.3 = (bf16[1,2,6,1,3072]{4,3,2,1,0:T(2,128)(2,1)S(1)}, bf16[1,2,6,1,3072]{4,3,2,1,0:T(2,128)(2,1)S(1)}, u32[]{:S(2)}, u32[]{:S(2)}) collective-permute-start(bf16[1,2,6,1,3072]{4,3,2,1,0:T(2,128)(2,1)S(1)} %get-tuple-element.92), channel_id=1, source_target_pairs={{1,0},{2,1},{3,2},{4,3},{5,4},{6,5},{7,6},{8,7},{9,8},{10,9},{11,1... | collective-permute-start | bytes 221192 | tf_op jit(solution)/shard_map/ppermute | solution.py:18
  62.2 7.0 %collective-permute-start.2 = (bf16[1,2,6,1,3072]{4,3,2,1,0:T(2,128)(2,1)S(1)}, bf16[1,2,6,1,3072]{4,3,2,1,0:T(2,128)(2,1)S(1)}, u32[]{:S(2)}, u32[]{:S(2)}) collective-permute-start(bf16[1,2,6,1,3072]{4,3,2,1,0:T(2,128)(2,1)S(1)} %get-tuple-element.91), channel_id=1, source_target_pairs={{0,1},{1,2},{2,3},{3,4},{4,5},{5,6},{6,7},{7,8},{8,9},{9,10},{10,1... | collective-permute-start | bytes 221192 | tf_op jit(solution)/shard_map/ppermute | solution.py:15
  64.2 10.6 %copy-start.3 = (f32[1,3072]{1,0:T(1,128)}, f32[1,3072]{1,0:T(1,128)S(1)}, u32[]{:S(2)}) copy-start(f32[1,3072]{1,0:T(1,128)S(1)} %get-tuple-element.107) | copy-start | bytes 36868
  74.8 84.4 %all-to-all-start = ((bf16[16,1,2,4,4,3072]{5,4,3,2,1,0:T(4,128)(2,1)}), bf16[16,1,2,4,4,3072]{5,4,3,2,1,0:T(4,128)(2,1)S(1)}, u32[]{:S(2)}, u32[]{:S(2)}) async-start(bf16[16,1,2,4,4,3072]{5,4,3,2,1,0:T(4,128)(2,1)} %stack.2), calls=%async_computation | async-start | bytes 6291456 | tf_op jit(solution)/shard_map/all_to_all | solution.py:85
  85.9 83.2 %all-gather.8.cloned.1.call-start = ((), (), s32[]{:S(2)}) async-start(), calls=%async_computation.1 | async-start | bytes 2433024 | tf_op jit(solution)/shard_map/all_gather | solution.py:93
  86.7 165.6 %all-gather.10.cloned.1.call-start = ((), (), s32[]{:S(2)}) async-start(), calls=%async_computation.2 | async-start | bytes 2228224 | tf_op jit(solution)/shard_map/all_gather | solution.py:113
  168.1 7.5 %copy-start.1 = (bf16[1,226,3072]{2,1,0:T(8,128)(2,1)S(1)}, bf16[1,226,3072]{2,1,0:T(8,128)(2,1)}, u32[]{:S(2)}) copy-start(bf16[1,226,3072]{2,1,0:T(8,128)(2,1)} %param.10) | copy-start | bytes 4165636
  173.2 3.1 copy-start.4
  174.0 154.2 %all-gather.12.cloned.1.call-start = ((), (), s32[]{:S(2)}) async-start(), calls=%async_computation.3 | async-start | bytes 2228224 | tf_op jit(solution)/shard_map/all_gather | solution.py:114
  174.7 1.7 copy-start.5
Sparse Core Ops, SparseCore 0:
  88.9 80.2 all-gather.7
  174.1 78.1 all-gather.9
  254.4 73.8 all-gather.11
